TPU v7x, 256 devices: a whole 4x4x8 slice. The times are simulated.
256 devices in a mesh: req: 4 (over y), vocab: 64 (over z, x, core).
Axes of the slice: x: 4, y: 4, z: 8, core: 2. Of those that a mesh axis runs over, the one named last changes fastest.
Arguments:
- hidden: bfloat16 [8192, 4096], P('req', 'vocab'), may hold values from -320 to 320
- gain: float32 [4096], replicated, may hold values from 0.5 to 1.5
- head: bfloat16 [4096, 32768], P(None, ('req', 'vocab'))
- targets: int32 [8192], P('req'), may hold values from 0 to 32767
- lengths: int32 [4, 4], P('req'), may hold values from 1 to 1280, 2048 in all within a row
Outputs:
- token_logprob: float32 [8192], P(('req', 'vocab'))
- token_entropy: float32 [8192], P(('req', 'vocab'))
- seq_logprob: float32 [12], P('req')
- seq_entropy: float32 [12], P('req')
Inputs may be any that keep to these rules, and one draw needn't show every extreme that they name: lengths[q, 3] counts the empty slots at the end of index q's rows.
All inputs are finite; a program needn't handle non-finite values.
Results may differ from a plain program's by a relative error of at most 0.0012.
Values may be sent and summed in bfloat16 or wider, within the bound.
A program may use at most 128 MiB of HBM per device.

v0:
```python
import jax
import jax.numpy as jnp
from jax import lax
from jax.sharding import Mesh
from jax.sharding import PartitionSpec as P

D = 4096
SEQ_DEV = 3
VOCAB = ("vocab_0", "vocab_1", "vocab_2")
REQ_VOCAB = ("req", "vocab_0", "vocab_1", "vocab_2")


EPS = 1e-05


def gathered_once(shard, axis):
    leaves = jax.tree.leaves(shard)
    order = sorted(range(len(leaves)), key=lambda k: -leaves[k].size)
    width = (1, *leaves[order[0]].shape)[-1]
    lines = [
        jnp.pad(leaves[k].reshape(-1), (0, -leaves[k].size % width)).reshape(-1, width)
        for k in order
    ]
    both, at, found = (lax.all_gather(jnp.concatenate(lines), axis), 0, {})
    for k, line in zip(order, lines):
        slab = both[:, at : at + len(line)].reshape(len(both), -1)
        found[k] = slab[:, : leaves[k].size].reshape(-1, *leaves[k].shape)
        at += len(line)
    numbers = iter(range(len(leaves)))
    return jax.tree.map(lambda _: found[next(numbers)], shard)


def combined_by_axis(shard, axes, combine):
    for axis in axes:
        pieces = gathered_once(shard, axis)
        shard = jax.tree.map(lambda part: part[0], pieces)
        for k in range(1, lax.axis_size(axis)):
            shard = combine(shard, jax.tree.map(lambda part: part[k], pieces))
    return shard


def combine_stats(first, second):
    peak = jnp.maximum(first[0], second[0])
    scale_first = jnp.exp(first[0] - peak)
    scale_second = jnp.exp(second[0] - peak)
    return (
        peak,
        first[1] * scale_first + second[1] * scale_second,
        first[2] * scale_first + second[2] * scale_second,
        first[3] + second[3],
    )


def finish_rows(peak, total, moment, picked):
    log_total = peak + jnp.log(total)
    return (picked - log_total, log_total - moment / total)


def shards(hidden, gain, head, targets, lengths):
    rows = hidden.shape[0]
    vocab_index = lax.axis_index(VOCAB)
    vocab_count = lax.axis_size(VOCAB)
    shard_cols = head.shape[1]
    width_cols = shard_cols * lax.axis_size("req")
    col_pos = jnp.arange(width_cols, dtype=jnp.int32)
    col_ids = (
        col_pos // shard_cols * (vocab_count * shard_cols)
        + vocab_index * shard_cols
        + col_pos % shard_cols
    )
    block = min(512, rows)
    count = rows // block
    seq_lens = lengths[0, :SEQ_DEV]
    ends = jnp.cumsum(seq_lens)
    starts = ends - seq_lens
    live = ends[-1]
    full_rows = lax.all_gather(hidden, VOCAB, axis=1, tiled=True)
    values = full_rows.astype(jnp.float32)
    mean_sq = jnp.sum(values * values, axis=1) / D
    normed = (values * lax.rsqrt(mean_sq + EPS)[:, None] * gain[None, :]).astype(jnp.bfloat16)
    columns = lax.all_gather(head, "req", axis=1, tiled=True)

    def block_logits(start):
        rows_blk = lax.dynamic_slice_in_dim(normed, start, block, 0)
        return jnp.dot(rows_blk, columns, preferred_element_type=jnp.float32)

    def compute_block(start):
        logits = block_logits(start)
        wanted = lax.dynamic_slice_in_dim(targets, start, block, 0)
        peak = jnp.max(logits, axis=1)
        weights = jnp.exp(logits - peak[:, None])
        total = jnp.sum(weights, axis=1)
        moment = jnp.sum(weights * logits, axis=1)
        picked = jnp.sum(jnp.where(col_ids[None, :] == wanted[:, None], logits, 0.0), axis=1)
        return (peak, total, moment, picked)

    def one_block(block_index):
        start = block_index * block
        return compute_block(start)

    peak, total, moment, picked = lax.map(one_block, jnp.arange(count, dtype=jnp.int32))
    peak = peak.reshape(rows)
    total = total.reshape(rows)
    moment = moment.reshape(rows)
    picked = picked.reshape(rows)
    share = rows // vocab_count
    divisor = seq_lens.astype(jnp.float32)
    peak, total, moment, picked = combined_by_axis(
        (peak, total, moment, picked), VOCAB, combine_stats
    )
    logprob, entropy = finish_rows(peak, total, moment, picked)
    local = jnp.arange(rows, dtype=jnp.int32)
    valid = local < live
    logprob = jnp.where(valid, logprob, 0.0)
    entropy = jnp.where(valid, entropy, 0.0)
    member = ((local[None, :] >= starts[:, None]) & (local[None, :] < ends[:, None])).astype(
        jnp.float32
    )
    seq_lp = jnp.sum(member * logprob[None, :], axis=1) / divisor
    seq_ent = jnp.sum(member * entropy[None, :], axis=1) / divisor
    own_lp = lax.dynamic_slice_in_dim(logprob, vocab_index * share, share, 0)
    own_ent = lax.dynamic_slice_in_dim(entropy, vocab_index * share, share, 0)
    return (own_lp, own_ent, seq_lp, seq_ent)


def solution(mesh):
    split = Mesh(
        mesh.devices.reshape(mesh.shape["req"], 8, 4, 2), ("req", "vocab_0", "vocab_1", "vocab_2")
    )
    placed = (P("req", VOCAB), P(), P(None, REQ_VOCAB), P("req"), P("req", None))
    return jax.shard_map(
        shards,
        mesh=split,
        in_specs=placed,
        out_specs=(P(REQ_VOCAB), P(REQ_VOCAB), P("req"), P("req")),
        check_vma=False,
    )
```

profile of v0, /device:TPU:1, one launch (start us, length us, event | category | flops | bytes accessed | tf_op | source)
XLA Modules:
  0.0 251.6 jit_solution(500161678944132281)
XLA Ops:
  7.2 0.7 all-gather.9.cloned.1.call-update
  8.0 0.7 all-gather.11.cloned.1.call-update
  8.7 0.7 slice_bitcast_fusion.36
  9.5 0.6 slice.300
  10.1 0.7 bitcast_subtract_fusion
  10.8 103.4 %all-gather.9.cloned.1.call-done = bf16[2048,4096]{0,1:T(8,128)(2,1)} async-done(((bf16[2048,64]{0,1:T(8,128)(2,1)}), bf16[2048,4096]{0,1:T(8,128)(2,1)}) %all-gather.9.cloned.1.call-update) | async-done | bytes 16777232 | tf_op jit(solution)/shard_map/all_gather | solution.py:77
  114.2 7.7 %fusion.16 = f32[2048]{0:T(1024)S(1)} fusion(bf16[2048,4096]{0,1:T(8,128)(2,1)} %all-gather.9.cloned.1.call-done), kind=kLoop, calls=%fused_computation.24 | loop fusion | flops 25163776 | bytes 16785408 | tf_op jit(solution)/shard_map/reduce_sum | solution.py:79
  121.9 3.4 %copy-done = bf16[2048,4096]{0,1:T(8,128)(2,1)S(1)} copy-done((bf16[2048,4096]{0,1:T(8,128)(2,1)S(1)}, bf16[2048,4096]{0,1:T(8,128)(2,1)}, u32[]{:S(2)}) %copy-start) | copy-done | bytes 16777240
  125.3 8.7 %fusion.18 = bf16[2048,4096]{0,1:T(8,128)(2,1)} fusion(bf16[2048,4096]{0,1:T(8,128)(2,1)S(1)} %copy-done, f32[4096]{0:T(1024)S(1)} %copy-done.1, f32[2048]{0:T(1024)S(1)} %add_rsqrt_fusion), kind=kLoop, calls=%fused_computation.26 | loop fusion | flops 33554432 | bytes 33579008 | tf_op jit(solution)/shard_map/convert_element_type | solution.py:80
  134.0 31.2 %all-gather.11.cloned.1.call-done = bf16[4096,512]{1,0:T(8,128)(2,1)} async-done(((bf16[4096,128]{1,0:T(8,128)(2,1)}), bf16[4096,512]{1,0:T(8,128)(2,1)}) %all-gather.11.cloned.1.call-update) | async-done | bytes 4194320 | tf_op jit(solution)/shard_map/all_gather | solution.py:81
  165.2 33.8 %while.17 = (s32[]{:T(128)}, f32[4,512]{1,0:T(4,128)S(1)}, f32[4,512]{1,0:T(4,128)S(1)}, f32[4,512]{1,0:T(4,128)S(1)}, f32[4,512]{1,0:T(4,128)S(1)}, /*index=5*/...) while((s32[]{:T(128)}, f32[4,512]{1,0:T(4,128)S(1)}, ...), condition=%wide.region_7.8_spmd.clone, body=%wide.region_2.7_spmd.clone.sunk | while | flops 2149586432 | bytes 10522843 | solution.py:101
  165.2 0.6 dynamic_slice.29
  166.5 5.9 %fusion.105 = (f32[512]{0:T(512)S(1)}, f32[512,512]{0,1:T(8,128)S(1)}) fusion(bf16[4096,512]{1,0:T(8,128)(2,1)} %get-tuple-element.256, bf16[2048,4096]{0,1:T(8,128)(2,1)} %get-tuple-element.255, s32[]{:T(128)S(6)} %select_n.72), kind=kOutput, calls=%fused_computation.187.clone.1 | convolution fusion | flops 2147745280 | bytes 9439236 | tf_op jit(solution)/shard_map/while/body/eval_jaxpr/dot_general | solution.py:85
  172.3 0.8 dynamic_slice.30
  173.7 0.6 dynamic_slice.29
  174.9 5.9 %fusion.105 = (f32[512]{0:T(512)S(1)}, f32[512,512]{0,1:T(8,128)S(1)}) fusion(bf16[4096,512]{1,0:T(8,128)(2,1)} %get-tuple-element.256, bf16[2048,4096]{0,1:T(8,128)(2,1)} %get-tuple-element.255, s32[]{:T(128)S(6)} %select_n.72), kind=kOutput, calls=%fused_computation.187.clone.1 | convolution fusion | flops 2147745280 | bytes 9439236 | tf_op jit(solution)/shard_map/while/body/eval_jaxpr/dot_general | solution.py:85
  180.8 0.8 dynamic_slice.30
  181.6 0.3 multiply_reduce_fusion.2
  182.1 0.6 dynamic_slice.29
  183.4 5.9 %fusion.105 = (f32[512]{0:T(512)S(1)}, f32[512,512]{0,1:T(8,128)S(1)}) fusion(bf16[4096,512]{1,0:T(8,128)(2,1)} %get-tuple-element.256, bf16[2048,4096]{0,1:T(8,128)(2,1)} %get-tuple-element.255, s32[]{:T(128)S(6)} %select_n.72), kind=kOutput, calls=%fused_computation.187.clone.1 | convolution fusion | flops 2147745280 | bytes 9439236 | tf_op jit(solution)/shard_map/while/body/eval_jaxpr/dot_general | solution.py:85
  189.2 0.8 dynamic_slice.30
  190.0 0.3 multiply_reduce_fusion.2
  190.6 0.6 dynamic_slice.29
  191.8 5.9 %fusion.105 = (f32[512]{0:T(512)S(1)}, f32[512,512]{0,1:T(8,128)S(1)}) fusion(bf16[4096,512]{1,0:T(8,128)(2,1)} %get-tuple-element.256, bf16[2048,4096]{0,1:T(8,128)(2,1)} %get-tuple-element.255, s32[]{:T(128)S(6)} %select_n.72), kind=kOutput, calls=%fused_computation.187.clone.1 | convolution fusion | flops 2147745280 | bytes 9439236 | tf_op jit(solution)/shard_map/while/body/eval_jaxpr/dot_general | solution.py:85
  197.7 0.8 dynamic_slice.30
  199.1 20.3 %all-gather.3 = f32[8,4,2048]{2,1,0:T(4,128)S(1)} all-gather(f32[1,4,2048]{2,1,0:T(4,128)S(1)} %maximum_bitcast_fusion), channel_id=2, replica_groups=mesh['req'=4,'vocab_0'=8,'vocab_1'=4,'vocab_2'=2] {'vocab_0'}, dimensions={0}, use_global_device_ids=true | all-gather | bytes 294912 | tf_op jit(solution)/shard_map/all_gather | solution.py:24
  219.9 9.4 %all-gather.4 = f32[4,4,2048]{2,1,0:T(4,128)S(1)} all-gather(f32[1,4,2048]{2,1,0:T(4,128)S(1)} %maximum_bitcast_fusion.1), channel_id=3, replica_groups=mesh['req'=4,'vocab_0'=8,'vocab_1'=4,'vocab_2'=2] {'vocab_1'}, dimensions={0}, use_global_device_ids=true | all-gather | bytes 163840 | tf_op jit(solution)/shard_map/all_gather | solution.py:24
  229.6 12.5 %all-gather.5 = f32[2,4,2048]{2,1,0:T(4,128)S(1)} all-gather(f32[1,4,2048]{2,1,0:T(4,128)S(1)} %maximum_bitcast_fusion.2), channel_id=4, replica_groups=mesh['req'=4,'vocab_0'=8,'vocab_1'=4,'vocab_2'=2] {'vocab_2'}, dimensions={0}, use_global_device_ids=true | all-gather | bytes 98304 | tf_op jit(solution)/shard_map/all_gather | solution.py:24
  242.1 0.7 subtract_select_fusion
  242.8 0.6 dynamic_slice.17
  243.4 0.6 dynamic_slice.16
  244.2 0.5 fusion.92
  (51 shorter events, 2.9 us)
Async XLA Ops:
  7.2 114.7 %copy-start.1 = (f32[4096]{0:T(1024)S(1)}, f32[4096]{0:T(1024)}, u32[]{:S(2)}) copy-start(f32[4096]{0:T(1024)} %param.8) | copy-start | bytes 49156
  7.2 107.0 %all-gather.9.cloned.1.call-start = ((), (), s32[]{:S(2)}) async-start(), calls=%async_computation | async-start | bytes 17039360 | tf_op jit(solution)/shard_map/all_gather | solution.py:77
  7.9 157.3 %all-gather.11.cloned.1.call-start = ((), (), s32[]{:S(2)}) async-start(), calls=%async_computation.1 | async-start | bytes 5242880 | tf_op jit(solution)/shard_map/all_gather | solution.py:81
  114.2 11.1 %copy-start = (bf16[2048,4096]{0,1:T(8,128)(2,1)S(1)}, bf16[2048,4096]{0,1:T(8,128)(2,1)}, u32[]{:S(2)}) copy-start(bf16[2048,4096]{0,1:T(8,128)(2,1)} %all-gather.9.cloned.1.call-done) | copy-start | bytes 50331652
  165.2 79.0 %copy-start.2 = (s32[1,4]{1,0:T(1,128)S(1)}, s32[1,4]{1,0:T(1,128)}, u32[]{:S(2)}) copy-start(s32[1,4]{1,0:T(1,128)} %param.11) | copy-start | bytes 52
Sparse Core Ops, SparseCore 0:
  10.8 103.3 all-gather.8
  116.0 49.1 all-gather.10
where the time goes:
time: 252 us
  waiting for transfers between devices  136 us (54%)
  blocking collectives  42.2 us (17%)
  matrix products  23.5 us (9%)
  other arithmetic  20.9 us (8%)
  between operations  14.2 us (6%)
  local copies, waits for them, and re-layouts  12.1 us (5%)
  loops' own time  2.75 us (1%)
    all_gather x1, waiting for transfers between devices, shards(): full_rows = lax.all_gather(hidden, VOCAB, axis=1, tiled=True)  103 us
    all_gather x3, blocking collectives, gathered_once(): both, at, found = (lax.all_gather(jnp.concatenate(lines), axis), 0, {})  42.2 us
    all_gather x1, waiting for transfers between devices, shards(): columns = lax.all_gather(head, 'req', axis=1, tiled=True)  31.2 us
    dot_general x4, matrix products, block_logits(): return jnp.dot(rows_blk, columns, preferred_element_type=jnp.float32)  23.5 us
    convert_element_type x1, other arithmetic, shards(): (values * lax.rsqrt(mean_sq + EPS)[:, None] * gain[None, :]).astype(jnp.b...  8.73 us
    reduce_sum x1, other arithmetic, shards(): mean_sq = jnp.sum(values * values, axis=1) / D  7.68 us
  transfers between devices with their start and end apart: 2, of which 2 were waited for; matrix products, arithmetic and copies ran while one was open for 7% of the time, Pallas kernels for 0%

commit v1 on v0

v1 whole, which is shorter than its diff:
```python
import jax
import jax.numpy as jnp
from jax import lax
from jax.experimental import pallas as pl
from jax.experimental.pallas import tpu as pltpu
from jax.sharding import Mesh
from jax.sharding import PartitionSpec as P

SEQ_DEV = 3
VOCAB = ("vocab_0", "vocab_1", "vocab_2")
REQ_VOCAB = ("req", "vocab_0", "vocab_1", "vocab_2")
EPS = 1e-05

NZ, NX, NY = 8, 4, 4
F32, BF16, I32 = jnp.float32, jnp.bfloat16, jnp.int32
FIRST = 48

GROUPS = (0, 1, -1, 2, -2, 3, -3, 4)
HEAD_FROM = (0, 1, -1, 2)

ARRIVALS = (
    (0, 0, 1), (0, 0, -1), (0, 1, 0), (0, -1, 0), (1, 0, 1), (1, 0, -1), (1, 1, 0), (1, -1, 0),
    (0, 0, 2), (0, 1, 1), (0, -1, 1), (0, 1, -1), (0, -1, -1), (1, 0, 2), (1, 1, -1), (0, 2, 0),
    (0, -2, 0), (1, 1, 1), (1, -1, -1), (1, 2, 0), (1, -2, 0), (1, -1, 1), (0, 1, 2), (0, -1, 2),
    (1, 1, 2), (0, 2, 1), (0, -2, 1), (1, 2, -1), (0, 2, -1), (0, -2, -1), (1, 2, 1), (0, 3, 0),
    (0, -3, 0), (1, -2, -1), (1, -2, 1), (1, -1, 2), (1, 3, 0), (1, -3, 0), (1, 2, 2), (0, 2, 2),
    (0, -2, 2), (0, 3, 1), (0, -3, 1), (1, -2, 2), (1, 3, -1), (0, 3, -1), (0, -3, -1), (1, 3, 1),
    (0, 4, 0), (0, -3, 2), (1, -3, -1), (1, 4, 0), (1, -3, 1), (0, 3, 2), (1, 3, 2), (0, 4, 1),
    (0, 4, -1), (0, 4, 2), (1, 4, 1), (1, 4, -1), (1, -3, 2), (1, 4, 2),
)
HIDDEN_AT = {name: i for i, name in enumerate(ARRIVALS)}


HEADS = ((0, 1), (2, 3), (4, 5), (6,), (), (7,), (), ())


def schedule():
    steps, pending = [], list(ARRIVALS)
    for t, dz in enumerate(GROUPS):
        last = max([i for i, name in enumerate(pending) if name[1] == dz], default=-1)
        here, pending = pending[: last + 1], pending[last + 1 :]
        heads = [("y", (s, dy)) for s in HEADS[t] for dy in (1, -1, 2)]
        placed = [(k / max(1, len(here)), ("h", name)) for k, name in enumerate(here)]
        placed += [((k + 1) / (len(heads) + 1), head) for k, head in enumerate(heads)]
        placed.sort(key=lambda item: item[0])
        steps.append([event for _, event in placed] + [("p", (t, dy)) for dy in HEAD_FROM])
    assert not pending
    return steps


def kernel(
    hid, gain, head, targets, lengths, out,
    H, W, acc, staged, squares, st_out, st_in, sx_out, sx_in, fin, fin_other,
    local_sem, hid_send, hid_recv, own_send, own_recv, y_send, y_recv, p_send, p_recv,
    z_send, z_recv, x_send, x_recv, f_send, f_recv, c_send, c_recv,
):
    y, z = lax.axis_index("req"), lax.axis_index("vocab_0")
    x, c = lax.axis_index("vocab_1"), lax.axis_index("vocab_2")
    way = 1 - 2 * c

    def at(y_to, z_to, x_to, c_to):
        return {"req": y_to, "vocab_0": z_to, "vocab_1": x_to, "vocab_2": c_to}

    def zof(d):
        return (z + NZ + way * d) % NZ

    def xof(d):
        return (x + NX + way * d) % NX

    def yof(d):
        return (y + NY + way * d) % NY

    partner = at(y, z, x, 1 - c)

    def remote(src, dst, send_sem, recv_sem, to):
        return pltpu.make_async_remote_copy(
            src_ref=src, dst_ref=dst, send_sem=send_sem, recv_sem=recv_sem,
            device_id=to, device_id_type=pl.DeviceIdType.MESH,
        )

    mine = pl.multiple_of(c * 1024, 1024)
    other = pl.multiple_of((1 - c) * 1024, 1024)
    own_rows = pl.ds(pl.multiple_of(c * 64, 64), 64)
    load_hid = pltpu.make_async_copy(
        hid.at[:, pl.ds(mine, 1024)], H.at[z, x, own_rows, :], local_sem.at[0]
    )
    load_head = pltpu.make_async_copy(head, staged, local_sem.at[1])
    load_hid.start()
    load_head.start()

    barrier = pltpu.get_barrier_semaphore()
    peers = [at(y, (z + k) % NZ, x, c) for k in range(1, NZ)]
    peers += [at(y, z, (x + k) % NX, c) for k in range(1, NX)]
    peers += [partner, at(yof(1), z, x, c), at(yof(-1), z, x, c)]
    for peer in peers:
        pl.semaphore_signal(barrier, inc=1, device_id=peer, device_id_type=pl.DeviceIdType.MESH)
    pl.semaphore_wait(barrier, len(peers))

    own_copy = remote(
        hid.at[:, pl.ds(other, 1024)], H.at[z, x, own_rows, :],
        own_send.at[0], own_recv.at[0], partner,
    )
    own_copy.start()
    load_hid.wait()
    own_copy.wait_recv()

    def piece(name):
        kind, dz, dx = name
        rows = pl.ds(0, FIRST) if kind == 0 else pl.ds(FIRST, 128 - FIRST)
        return H.at[zof(-dz), xof(-dx), rows, :]

    def hidden_copy(name, hop):
        kind, dz, dx = name
        ez, ex = hop
        k = HIDDEN_AT[(kind, dz + ez, dx + ex)]
        to = at(y, zof(ez), xof(ex), c)
        return remote(piece(name), piece(name), hid_send.at[k], hid_recv.at[k], to)

    def hops(name):
        kind, dz, dx = name
        along_x = [(0, 1), (0, -1)] if dx == 0 else [(0, 1)] if dx == 1 else []
        along_z = [(1, 0), (-1, 0)] if dz == 0 else [(1, 0)] if 0 < dz < 4 else []
        along_z = [(-1, 0)] if dz in (-1, -2) else along_z
        if kind == 0:
            return (along_x if dz == 0 else []) + along_z
        return (along_z if dx == 0 else []) + along_x

    def forward(name):
        for hop in hops(name):
            hidden_copy(name, hop).start()

    def take_hidden(name):
        k = HIDDEN_AT[name]
        remote(piece(name), piece(name), hid_send.at[k], hid_recv.at[k], partner).wait_recv()
        forward(name)

    forward((1, 0, 0))
    forward((0, 0, 0))

    load_head.wait()
    own_cols = y * 2 + c

    def stage(s, carry):
        cols = pl.ds(pl.multiple_of(s * 512, 512), 512)
        block = staged[cols, :].astype(F32).T
        W[own_cols, s] = (block * (gain[:, cols] * (2.0 ** -9))).astype(BF16)
        return carry

    lax.fori_loop(0, 8, stage, 0)

    def slab(t, dy, core):
        return W.at[yof(-dy) * 2 + core, zof(-GROUPS[t])]

    def y_index(t, dy):
        return t * 3 + (0, 1, 2)[(1, -1, 2).index(dy)]

    def send_y(t, dy, hop):
        k = y_index(t, dy + hop)
        to = at(yof(hop), z, x, c)
        return remote(slab(t, dy, c), slab(t, dy, c), y_send.at[k], y_recv.at[k], to)

    def send_p(t, dy):
        mirror = GROUPS.index(-GROUPS[t]) if abs(GROUPS[t]) < 4 else t
        k = mirror * 4 + HEAD_FROM.index(-dy if dy < 2 else dy)
        return remote(slab(t, dy, c), slab(t, dy, c), p_send.at[k], p_recv.at[k], partner)

    def own_slab(t):
        send_y(t, 0, 1).start()
        send_y(t, 0, -1).start()
        send_p(t, 0).start()

    def take_y(t, dy):
        k = y_index(t, dy)
        ref = slab(t, dy, c)
        remote(ref, ref, y_send.at[k], y_recv.at[k], partner).wait_recv()
        if dy == 1:
            send_y(t, 1, 1).start()
            if t + 2 < 8:
                own_slab(t + 2)
        send_p(t, dy).start()

    def take_p(t, dy):
        k = t * 4 + HEAD_FROM.index(dy)
        ref = slab(t, dy, 1 - c)
        remote(ref, ref, p_send.at[k], p_recv.at[k], partner).wait_recv()

    own_slab(0)
    own_slab(1)

    acc[...] = jnp.zeros((1024, 1024), F32)
    squares[...] = jnp.zeros((8, 1024), F32)
    steps = schedule()

    def step(t, carry):
        for k, events in enumerate(steps):

            @pl.when(t == k)
            def _():
                for kind, what in events:
                    {"h": take_hidden, "y": lambda w: take_y(*w), "p": lambda w: take_p(*w)}[kind](what)

        sign = 1 - 2 * (t % 2)
        group = (z + 2 * NZ + way * sign * ((t + 1) // 2)) % NZ

        acc[...] += jnp.dot(
            W[:, group].reshape(1024, 512), H[group].reshape(512, 1024),
            preferred_element_type=F32,
        )

        def square(i, total):
            v = H[group, i // 4, pl.ds(pl.multiple_of((i % 4) * 32, 32), 32), :].astype(F32)
            return total + jnp.sum((v * v).reshape(4, 8, 1024), axis=0)

        squares[...] = lax.fori_loop(0, 16, square, squares[...])
        return carry

    lax.fori_loop(0, 8, step, 0)

    mean_sq = jnp.sum(squares[...], axis=0, keepdims=True) / 4096.0
    scale = lax.rsqrt(mean_sq + EPS) * 512.0

    def highest(i, best):
        v = acc[pl.ds(pl.multiple_of(i * 32, 32), 32), :]
        return jnp.maximum(best, jnp.max(v.reshape(4, 8, 1024), axis=0))

    top = lax.fori_loop(1, 32, highest, jnp.max(acc[0:32, :].reshape(4, 8, 1024), axis=0))
    peak = jnp.max(top, axis=0, keepdims=True) * scale
    wanted = targets[:, pl.ds(mine, 1024)]
    in_y = wanted // 8192
    in_p = (wanted // 256) % 32
    local = jnp.where(in_p == z * 4 + x, in_y * 256 + wanted % 256, -1)
    for part in range(4):
        lanes = slice(part * 256, part * 256 + 256)
        scale_b = jnp.broadcast_to(scale[:, lanes], (8, 256))
        peak_b = jnp.broadcast_to(peak[:, lanes], (8, 256))
        local_b = jnp.broadcast_to(local[:, lanes], (8, 256)) - lax.broadcasted_iota(I32, (8, 256), 0)

        def sums(i, carry):
            total, moment, picked = carry
            for j in range(4):
                row = pl.multiple_of(i * 32 + j * 8, 8)
                logit = acc[pl.ds(row, 8), lanes] * scale_b
                weight = jnp.exp(logit - peak_b)
                total = total + weight
                moment = moment + weight * logit
                picked = picked + jnp.where(local_b == row, logit, 0.0)
            return total, moment, picked

        zero = jnp.zeros((8, 256), F32)
        total, moment, picked = lax.fori_loop(0, 32, sums, (zero, zero, zero))
        for k in range(2):
            cut = slice(k * 128, k * 128 + 128)
            for row, value in enumerate((total, moment, picked)):
                st_out[part * 2 + k, row + 1 : row + 2, :] = jnp.sum(value[:, cut], axis=0, keepdims=True)
            st_out[part * 2 + k, 0:1, :] = peak[:, part * 256 + k * 128 : part * 256 + k * 128 + 128]

    def combine(tiles):
        tops = tiles[:, 0, :]
        most = jnp.max(tops, axis=0, keepdims=True)
        factor = jnp.exp(tops - most)
        return (
            most,
            jnp.sum(tiles[:, 1, :] * factor, axis=0, keepdims=True),
            jnp.sum(tiles[:, 2, :] * factor, axis=0, keepdims=True),
            jnp.sum(tiles[:, 3, :], axis=0, keepdims=True),
        )

    def z_copy(k):
        return remote(
            st_out.at[(z + k) % NZ], st_in.at[z], z_send.at[k], z_recv.at[k], at(y, (z + k) % NZ, x, c)
        )

    for k in range(1, NZ):
        z_copy(k).start()
    st_in[z] = st_out[z]
    for k in range(1, NZ):
        ref = st_in.at[(z + NZ - k) % NZ]
        remote(ref, ref, z_send.at[k], z_recv.at[k], partner).wait_recv()
    for row, value in enumerate(combine(st_in)):
        sx_out[row : row + 1, :] = value

    def x_copy(k):
        return remote(
            sx_out, sx_in.at[x], x_send.at[k], x_recv.at[k], at(y, z, (x + k) % NX, c)
        )

    for k in range(1, NX):
        x_copy(k).start()
    sx_in[x] = sx_out[...]
    for k in range(1, NX):
        ref = sx_in.at[(x + NX - k) % NX]
        remote(ref, ref, x_send.at[k], x_recv.at[k], partner).wait_recv()
    top_all, total_all, moment_all, picked_all = combine(sx_in)
    log_total = top_all + jnp.log(total_all)
    lens = [lengths[0, k] for k in range(SEQ_DEV)]
    ends = [lens[0], lens[0] + lens[1], lens[0] + lens[1] + lens[2]]
    row_ids = c * 1024 + z * 128 + lax.broadcasted_iota(I32, (1, 128), 1)
    valid = row_ids < ends[2]
    fin[z, 0:1, :] = jnp.where(valid, picked_all - log_total, 0.0)
    fin[z, 1:2, :] = jnp.where(valid, log_total - moment_all / total_all, 0.0)

    def f_copy(k):
        return remote(fin.at[z], fin.at[z], f_send.at[k], f_recv.at[k], at(y, (z + k) % NZ, x, c))

    for k in range(1, NZ):
        f_copy(k).start()
    for k in range(1, NZ):
        ref = fin.at[(z + NZ - k) % NZ]
        remote(ref, ref, f_send.at[k], f_recv.at[k], partner).wait_recv()
    c_copy = remote(fin, fin_other, c_send.at[0], c_recv.at[0], partner)
    c_copy.start()
    c_copy.wait_recv()

    lane = lax.broadcasted_iota(I32, (1, 128), 1)
    tile = ((z % 4) * 4 + x) // 2
    shift = (128 - (64 * (x % 2) + 32 * c)) % 128
    here = jnp.where(z // 4 == c, fin[tile], fin_other[tile])
    out[...] = pltpu.roll(here, shift, 1)
    ids = lax.broadcasted_iota(I32, (8, 128), 0) * 128 + lax.broadcasted_iota(I32, (8, 128), 1)
    for row in range(2):
        line = jnp.zeros((1, 128), F32)
        for k in range(SEQ_DEV):
            start = ends[k] - lens[k]
            parts = []
            for values, first in ((fin[:, row, :], mine), (fin_other[:, row, :], other)):
                rows = ids + first
                inside = (rows >= start) & (rows < ends[k])
                kept = jnp.where(inside, values, 0.0)
                parts.append(jnp.sum(jnp.sum(kept, axis=0, keepdims=True), axis=1, keepdims=True))
            mean = (parts[0] + parts[1]) / jnp.broadcast_to(lens[k].astype(F32), (1, 1))
            line = jnp.where(lane == k, mean, line)
        out[2 + row : 3 + row, :] = line

    own_copy.wait_send()
    for name in [(0, 0, 0), (1, 0, 0), *ARRIVALS]:
        for hop in hops(name):
            hidden_copy(name, hop).wait_send()
    for t in range(8):
        send_y(t, 0, 1).wait_send()
        send_y(t, 0, -1).wait_send()
        send_y(t, 1, 1).wait_send()
        for dy in HEAD_FROM:
            send_p(t, dy).wait_send()
    for k in range(1, NZ):
        z_copy(k).wait_send()
        f_copy(k).wait_send()
    for k in range(1, NX):
        x_copy(k).wait_send()
    c_copy.wait_send()


def shards(hidden, gain, head, targets, lengths):
    dma = pltpu.SemaphoreType.DMA
    n = len(ARRIVALS)
    vmem = pl.BlockSpec(memory_space=pltpu.VMEM)
    tile = pl.pallas_call(
        kernel,
        out_shape=jax.ShapeDtypeStruct((8, 128), F32),
        in_specs=[
            pl.BlockSpec(memory_space=pl.ANY), vmem, pl.BlockSpec(memory_space=pl.ANY), vmem,
            pl.BlockSpec(memory_space=pltpu.SMEM),
        ],
        out_specs=vmem,
        scratch_shapes=[
            pltpu.VMEM((NZ, NX, 128, 1024), BF16),
            pltpu.VMEM((8, 8, 128, 512), BF16),
            pltpu.VMEM((1024, 1024), F32),
            pltpu.VMEM((4096, 128), BF16),
            pltpu.VMEM((8, 1024), F32),
            pltpu.VMEM((NZ, 8, 128), F32),
            pltpu.VMEM((NZ, 8, 128), F32),
            pltpu.VMEM((8, 128), F32),
            pltpu.VMEM((NX, 8, 128), F32),
            pltpu.VMEM((NZ, 8, 128), F32),
            pltpu.VMEM((NZ, 8, 128), F32),
            dma((2,)), dma((n,)), dma((n,)), dma((1,)), dma((1,)), dma((24,)), dma((24,)),
            dma((32,)), dma((32,)), dma((8,)), dma((8,)), dma((4,)), dma((4,)), dma((8,)), dma((8,)),
            dma((1,)), dma((1,)),
        ],
        compiler_params=pltpu.CompilerParams(
            collective_id=0, has_side_effects=True, vmem_limit_bytes=48 * 1024 * 1024
        ),
        name="rollout_stats",
    )(hidden.T, gain.reshape(1, 4096), head, targets.reshape(1, 2048), lengths)
    return tile[0, :32], tile[1, :32], tile[2, :SEQ_DEV], tile[3, :SEQ_DEV]


def solution(mesh):
    split = Mesh(
        mesh.devices.reshape(mesh.shape["req"], NZ, NX, 2), ("req", "vocab_0", "vocab_1", "vocab_2")
    )
    placed = (P("req", VOCAB), P(), P(None, REQ_VOCAB), P("req"), P("req", None))
    return jax.shard_map(
        shards,
        mesh=split,
        in_specs=placed,
        out_specs=(P(REQ_VOCAB), P(REQ_VOCAB), P("req"), P("req")),
        check_vma=False,
    )
```

time: 252 us -> 100 us (0.40)
  waiting for transfers between devices: 136 us -> 0 us
  Pallas kernels: 0 us -> 94.2 us
  blocking collectives: 42.2 us -> 0 us
  matrix products: 23.5 us -> 0 us
  other arithmetic: 20.9 us -> 0 us
  between operations: 14.2 us -> 0.65 us
  local copies, waits for them, and re-layouts: 12.1 us -> 5.27 us
  loops' own time: 2.75 us -> 0 us
    all_gather x2 -> x0, waiting for transfers between devices: 135 us -> none  [the longest x1 103 us: shards(): full_rows = lax.all_gather(hidden, VOCAB, axis=1, tiled=True)]
    pallas_call x0 -> x1, Pallas kernels: none -> 94.2 us  [shards(): pl.pallas_call(kernel, out_shape=jax.ShapeDtypeStruct((8, 128), F32), in_...]
    all_gather x3 -> x0, blocking collectives: 42.2 us -> none  [gathered_once(): both, at, found = (lax.all_gather(jnp.concatenate(lines), axis), 0, {})]
    dot_general x4 -> x0, matrix products: 23.5 us -> none  [block_logits(): return jnp.dot(rows_blk, columns, preferred_element_type=jnp.float32)]
    reduce_sum x6 -> x0, other arithmetic: 9.25 us -> none  [the longest x1 7.68 us: shards(): mean_sq = jnp.sum(values * values, axis=1) / D]
    convert_element_type x1 -> x0, other arithmetic: 8.73 us -> none  [shards(): (values * lax.rsqrt(mean_sq + EPS)[:, None] * gain[None, :]).astype(jnp.b...]
    dynamic_slice x10 -> x0, local copies, waits for them, and re-layouts: 6.58 us -> none  [the longest x4 3.06 us: compute_block(): wanted = lax.dynamic_slice_in_dim(targets, start, block, 0)]
    another operation x1 -> x0, loops' own time: 2.75 us -> none  [shards(): lax.map(one_block, jnp.arange(count, dtype=jnp.int32))]
  transfers between devices with their start and end apart: 2 -> 0, of which waited for: 2 -> 0; matrix products, arithmetic and copies ran while one was open for 7% -> 0% of each run, Pallas kernels for 0% -> 0%
where the time goes in v1:
time: 100 us
  Pallas kernels  94.2 us (94%)
  local copies, waits for them, and re-layouts  5.27 us (5%)
    pallas_call x1, Pallas kernels, shards(): pl.pallas_call(kernel, out_shape=jax.ShapeDtypeStruct((8, 128), F32), in_...  94.2 us
    unnamed x10, local copies, waits for them, and re-layouts  4.24 us

profile of v1, /device:TPU:1, one launch (start us, length us, event | category | flops | bytes accessed | tf_op | source)
XLA Modules:
  0.0 100.1 jit_solution(2633536663340050166)
XLA Ops:
  0.6 0.0 copy-start.4
  0.6 0.6 copy-done.4
  1.3 0.0 copy-start
  1.3 1.2 %copy-done = bf16[4096,128]{1,0:T(8,128)(2,1)S(1)} copy-done((bf16[4096,128]{1,0:T(8,128)(2,1)S(1)}, bf16[4096,128]{1,0:T(8,128)(2,1)}, u32[]{:S(2)}) %copy-start) | copy-done | bytes 1048600
  2.5 0.0 copy-start.1
  2.5 0.9 copy-done.1
  3.5 0.0 copy-start.2
  3.5 0.7 copy-done.2
  4.2 0.0 copy-start.3
  4.2 0.7 copy-done.3
  4.9 94.2 %rollout_stats.1 = f32[8,128]{1,0:T(8,128)S(1)} custom-call(bf16[64,2048]{1,0:T(8,128)(2,1)S(1)} %bitcast.11, f32[1,4096]{1,0:T(1,128)S(1)} %bitcast.12, bf16[4096,128]{1,0:T(8,128)(2,1)S(1)} %copy-done, s32[1,2048]{1,0:T(1,128)S(1)} %bitcast.13, s32[1,4]{1,0:T(1,128)S(1)} %copy-done.4), custom_call_target="tpu_custom_call" | custom-call | tf_op jit(solution)/shard_map/rollout_stats/pallas_call | solution.py:356
  99.1 0.5 slice_bitcast_fusion
  99.6 0.5 slice_bitcast_fusion.2
Async XLA Ops:
  0.6 0.7 copy-start.4
  1.3 1.2 %copy-start = (bf16[4096,128]{1,0:T(8,128)(2,1)S(1)}, bf16[4096,128]{1,0:T(8,128)(2,1)}, u32[]{:S(2)}) copy-start(bf16[4096,128]{1,0:T(8,128)(2,1)} %head.1) | copy-start | bytes 3145732
  2.5 0.9 copy-start.1
  3.5 0.7 copy-start.2
  4.2 0.7 copy-start.3
